TPU v7x, 32 devices: a whole 2x2x4 slice. The times are simulated.
32 devices in a mesh: dp: 8 (over z, y), tensor: 4 (over x, core).
Axes of the slice: x: 2, y: 2, z: 4, core: 2. Of those that a mesh axis runs over, the one named last changes fastest.
Arguments:
- gradients: bfloat16 [8, 2, 256, 1792], P('dp', None, None, 'tensor'), may hold values from -16 to 16, as said below
- errors: float32 [8, 2, 256, 1792], P('dp', None, None, 'tensor'), may hold values from -4 to 4
- start_factors: float32 [2, 1792, 32], P(None, 'tensor'), may hold values from -5 to 5
- moments: float32 [2, 256, 1792], P(None, 'dp', 'tensor'), may hold values from -2 to 2
- weights: float32 [2, 256, 1792], P(None, 'dp', 'tensor'), may hold values from -5 to 5
- vector_grads: bfloat16 [8, 5, 1792], P('dp', None, 'tensor'), may hold values from -16 to 16, as said below
- vector_moments: float32 [5, 1792], P(None, 'tensor'), may hold values from -2 to 2
- vector_weights: float32 [5, 1792], P(None, 'tensor'), may hold values from 0.5 to 1.5
Outputs:
- new_errors: float32 [8, 2, 256, 1792], P('dp', None, None, 'tensor')
- new_moments: float32 [2, 256, 1792], P(None, 'dp', 'tensor')
- new_weights: bfloat16 [2, 256, 1792], P(None, None, 'tensor')
- new_vector_moments: float32 [5, 1792], P(None, 'tensor')
- new_vector_weights: float32 [5, 1792], P(None, 'tensor')
Inputs may be any that keep to these rules, and one draw needn't show every extreme that they name: `gradients`: each replica's gradient is a part common to all replicas plus its own part. `vector_grads`: each replica's gradient is a part common to all replicas plus its own part.
All inputs are finite; a program needn't handle non-finite values.
Results may differ from a plain program's by a relative error of at most 0.0004.
Values may be sent and summed in bfloat16 or wider, within the bound.
A program may use at most 64 MiB of HBM per device.

v0:
```python
import jax
import jax.numpy as jnp
from jax import lax
from jax.sharding import PartitionSpec as P

ROUNDS = 2


momentum_coef = 0.9
step_rate = 0.1


def basis_from(gram_mat, summed):
    factor_low = jnp.linalg.cholesky(gram_mat)
    return lax.linalg.triangular_solve(
        factor_low, summed, left_side=False, lower=True, transpose_a=True
    )


def left_basis(mixed, right_f):
    partial_value = jnp.einsum("mkd,mdr->mkr", mixed, right_f, precision=lax.Precision.HIGHEST)
    summed = lax.psum(partial_value, ("dp", "tensor"))
    gram_mat = jnp.einsum("mkr,mks->mrs", summed, summed, precision=lax.Precision.HIGHEST)
    return basis_from(gram_mat, summed)


def update(mixed, start, moments, weights):
    right_f = start
    for round_idx in range(ROUNDS):
        basis_now = left_basis(mixed, right_f)
        right_part = jnp.einsum("mkd,mkr->mdr", mixed, basis_now, precision=lax.Precision.HIGHEST)
        right_f = lax.psum(right_part, "dp")
    replicas = lax.axis_size("dp")
    approx = (
        jnp.einsum("mkr,mdr->mkd", basis_now, right_f, precision=lax.Precision.HIGHEST) / replicas
    )
    fresh_errors = mixed - approx
    own_rows = moments.shape[1]
    my_rows = lax.dynamic_slice_in_dim(approx, lax.axis_index("dp") * own_rows, own_rows, 1)
    fresh_moments = momentum_coef * moments + my_rows
    fresh_weights = (weights - step_rate * fresh_moments).astype(jnp.bfloat16)
    regathered = lax.all_gather(fresh_weights, "dp", axis=1, tiled=True)
    return (fresh_errors, fresh_moments, regathered)


def per_device(
    gradients, errors, start_factors, moments, weights, vector_grads, vector_moments, vector_weights
):
    mixed = gradients[0].astype(jnp.float32) + errors[0]
    fresh_errors, fresh_moments, regathered = update(mixed, start_factors, moments, weights)
    vector_total = lax.psum(vector_grads[0].astype(jnp.float32), "dp")
    vector_mean = vector_total / lax.axis_size("dp")
    fresh_vector_moments = momentum_coef * vector_moments + vector_mean
    fresh_vector_weights = vector_weights - step_rate * fresh_vector_moments
    return (
        fresh_errors[None],
        fresh_moments,
        regathered,
        fresh_vector_moments,
        fresh_vector_weights,
    )


def solution(mesh):
    in_specs = (
        P("dp", None, None, "tensor"),
        P("dp", None, None, "tensor"),
        P(None, "tensor", None),
        P(None, "dp", "tensor"),
        P(None, "dp", "tensor"),
        P("dp", None, "tensor"),
        P(None, "tensor"),
        P(None, "tensor"),
    )
    out_specs = (
        P("dp", None, None, "tensor"),
        P(None, "dp", "tensor"),
        P(None, None, "tensor"),
        P(None, "tensor"),
        P(None, "tensor"),
    )
    return jax.shard_map(
        per_device, mesh=mesh, in_specs=in_specs, out_specs=out_specs, check_vma=False
    )
```

profile of v0, /device:TPU:0, one launch (start us, length us, event | category | flops | bytes accessed | tf_op | source)
XLA Modules:
  0.0 471.9 jit_solution(15930844537223940268)
XLA Ops:
  7.2 0.8 copy-done
  8.1 2.6 fusion.6
  10.8 123.7 %all-reduce.5.cloned.1.call-done = f32[2,256,32]{1,2,0:T(8,128)} async-done(((f32[2,256,32]{1,2,0:T(8,128)}), f32[2,256,32]{1,2,0:T(8,128)}) %all-reduce.5.cloned.1.call-update) | async-done | bytes 65552 | tf_op jit(solution)/shard_map/psum | solution.py:22
  134.5 1.1 fusion.13
  135.7 5.9 %custom-call.8 = f32[2,32,32]{2,1,0:T(8,128)S(1)} custom-call(f32[2,32,32]{2,1,0:T(8,128)S(1)} %fusion.12), custom_call_target="Cholesky" | custom-call | tf_op jit(solution)/shard_map/jit(cholesky)/cholesky | solution.py:14
  141.8 4.9 %custom-call.9 = f32[2,1,32,32]{2,3,1,0:T(8,128)S(1)} custom-call(f32[2,1,32,32]{3,2,1,0:T(8,128)S(1)} %select_bitcast_fusion.1), custom_call_target="InvertDiagBlocksLowerTriangular" | custom-call | tf_op jit(solution)/shard_map/triangular_solve/custom-call.0 | solution.py:15
  146.7 1.1 convolution_bitcast_fusion.1
  147.8 1.6 fusion.4
  149.5 70.5 %all-reduce.7.cloned.1.call-done = f32[2,448,32]{1,2,0:T(8,128)} async-done(((f32[2,448,32]{1,2,0:T(8,128)}), f32[2,448,32]{1,2,0:T(8,128)}) %all-reduce.7.cloned.1.call-update) | async-done | bytes 114704 | tf_op jit(solution)/shard_map/psum | solution.py:32
  220.0 2.3 fusion.2
  223.2 0.7 copy-done.5
  224.1 35.5 %psum.39 = f32[5,448]{1,0:T(8,128)S(1)} all-reduce(f32[5,448]{1,0:T(8,128)S(1)} %bitcast_convert_fusion), channel_id=1, replica_groups=mesh['dp'=8,'tensor'=4] {'dp'}, use_global_device_ids=true, to_apply=%region_6.9 | all-reduce | flops 2240 | bytes 17920 | tf_op jit(solution)/shard_map/psum | solution.py:51
  259.6 84.4 %all-reduce.9.cloned.1.call-done = f32[2,256,32]{1,2,0:T(8,128)} async-done(((f32[2,256,32]{1,2,0:T(8,128)}), f32[2,256,32]{1,2,0:T(8,128)}) %all-reduce.9.cloned.1.call-update) | async-done | bytes 65552 | tf_op jit(solution)/shard_map/psum | solution.py:22
  344.0 1.1 fusion.14
  345.2 5.9 %custom-call.10 = f32[2,32,32]{2,1,0:T(8,128)S(1)} custom-call(f32[2,32,32]{2,1,0:T(8,128)S(1)} %fusion.10), custom_call_target="Cholesky" | custom-call | tf_op jit(solution)/shard_map/jit(cholesky)/cholesky | solution.py:14
  351.3 4.9 %custom-call.11 = f32[2,1,32,32]{2,3,1,0:T(8,128)S(1)} custom-call(f32[2,1,32,32]{3,2,1,0:T(8,128)S(1)} %select_bitcast_fusion), custom_call_target="InvertDiagBlocksLowerTriangular" | custom-call | tf_op jit(solution)/shard_map/triangular_solve/custom-call.0 | solution.py:15
  356.5 1.6 fusion
  358.1 0.7 copy-done.6
  359.4 69.2 %all-reduce.11.cloned.1.call-done = f32[2,448,32]{1,2,0:T(8,128)} async-done(((f32[2,448,32]{1,2,0:T(8,128)}), f32[2,448,32]{1,2,0:T(8,128)}) %all-reduce.11.cloned.1.call-update) | async-done | bytes 114704 | tf_op jit(solution)/shard_map/psum | solution.py:32
  428.7 1.8 convolution_multiply_fusion
  430.5 1.1 fusion.8
  431.9 0.8 copy.34
  432.8 31.5 %all_gather.3 = bf16[2,256,448]{2,0,1:T(2,128)(2,1)S(1)} all-gather(bf16[2,32,448]{2,0,1:T(2,128)(2,1)S(1)} %copy.33), channel_id=1, replica_groups=mesh['dp'=8,'tensor'=4] {'dp'}, dimensions={1}, use_global_device_ids=true | all-gather | bytes 516096 | tf_op jit(solution)/shard_map/all_gather | solution.py:42
  464.3 1.1 copy.35
  (42 shorter events, 3.1 us)
Async XLA Ops:
  7.2 0.9 copy-start
  7.2 140.6 %copy-start.1 = (f32[1,2,256,448]{2,3,1,0:T(8,128)S(1)}, f32[1,2,256,448]{2,3,1,0:T(8,128)}, u32[]{:S(2)}) copy-start(f32[1,2,256,448]{2,3,1,0:T(8,128)} %param.12) | copy-start | bytes 2752516
  7.2 127.3 %all-reduce.5.cloned.1.call-start = ((), (), s32[]{:S(2)}) async-start(), calls=%async_computation | async-start | bytes 131072 | tf_op jit(solution)/shard_map/psum | solution.py:22
  10.7 137.1 %copy-start.2 = (bf16[1,2,256,448]{2,3,1,0:T(8,128)(2,1)S(1)}, bf16[1,2,256,448]{2,3,1,0:T(8,128)(2,1)}, u32[]{:S(2)}) copy-start(bf16[1,2,256,448]{2,3,1,0:T(8,128)(2,1)} %param.11) | copy-start | bytes 1376260
  10.7 209.3 %all-reduce.7.cloned.1.call-start = ((), (), s32[]{:S(2)}) async-start(), calls=%async_computation.1 | async-start | bytes 262144 | tf_op jit(solution)/shard_map/psum | solution.py:32
  149.5 194.5 %all-reduce.9.cloned.1.call-start = ((), (), s32[]{:S(2)}) async-start(), calls=%async_computation.2 | async-start | bytes 131072 | tf_op jit(solution)/shard_map/psum | solution.py:22
  220.0 3.0 copy-start.4
  222.3 0.7 copy-start.8
  222.3 206.3 %all-reduce.11.cloned.1.call-start = ((), (), s32[]{:S(2)}) async-start(), calls=%async_computation.3 | async-start | bytes 262144 | tf_op jit(solution)/shard_map/psum | solution.py:32
  223.0 0.9 copy-start.5
  345.1 11.0 %copy-start.3 = (f32[2,256,32]{1,2,0:T(8,128)S(1)}, f32[2,256,32]{1,2,0:T(8,128)}, u32[]{:S(2)}) copy-start(f32[2,256,32]{1,2,0:T(8,128)} %all-reduce.9.cloned.1.call-done) | copy-start | bytes 196612
  358.1 0.7 copy-start.6
  358.1 0.7 copy-start.7
Sparse Core Ops, SparseCore 0:
  14.2 120.2 all-reduce.4
  149.6 70.3 all-reduce.6
  227.1 116.7 all-reduce.8
  358.2 70.3 all-reduce.10
where the time goes:
time: 472 us
  waiting for transfers between devices  348 us (74%)
  blocking collectives  67 us (14%)
  other arithmetic  23.9 us (5%)
  between operations  13.9 us (3%)
  matrix products  13.6 us (3%)
  local copies, waits for them, and re-layouts  5.47 us (1%)
    psum x2, waiting for transfers between devices, left_basis(): summed = lax.psum(partial_value, ('dp', 'tensor'))  208 us
    psum x2, waiting for transfers between devices, update(): right_f = lax.psum(right_part, 'dp')  140 us
    psum x1, blocking collectives, per_device(): vector_total = lax.psum(vector_grads[0].astype(jnp.float32), 'dp')  35.5 us
    all_gather x1, blocking collectives, update(): regathered = lax.all_gather(fresh_weights, 'dp', axis=1, tiled=True)  31.5 us
    another operation x7, other arithmetic, basis_from(): factor_low = jnp.linalg.cholesky(gram_mat)  12 us
    another operation x5, other arithmetic, basis_from(): lax.linalg.triangular_solve(factor_low, summed, left_side=False, lower=Tr...  9.99 us
  transfers between devices with their start and end apart: 4, of which 4 were waited for; matrix products, arithmetic and copies ran while one was open for 0% of the time, Pallas kernels for 0%

commit v1 on v0

--- a/solution.py
+++ b/solution.py
@@ -1,9 +1,15 @@
+import functools
+
 import jax
 import jax.numpy as jnp
 from jax import lax
+from jax.experimental import pallas as pl
+from jax.experimental.pallas import tpu as pltpu
 from jax.sharding import PartitionSpec as P
 
 ROUNDS = 2
+LANES = 128
+MESH = pl.DeviceIdType.MESH
 
 
 momentum_coef = 0.9
@@ -61,6 +67,358 @@
     )
 
 
+def split(x):
+    high = x.astype(jnp.bfloat16)
+    low = (x - high.astype(jnp.float32)).astype(jnp.bfloat16)
+    return high, low
+
+
+def product(x, high, low, dims):
+    rows = x.shape[0]
+    both = jnp.concatenate(split(x), axis=0)
+    dot = functools.partial(
+        lax.dot_general, dimension_numbers=(dims, ((), ())), preferred_element_type=jnp.float32
+    )
+    out = dot(both, high) + dot(both, low)
+    return out[:rows] + out[rows:]
+
+
+def exact_dot(x, y, dims):
+    return lax.dot_general(
+        x,
+        y,
+        (dims, ((), ())),
+        precision=lax.Precision.HIGHEST,
+        preferred_element_type=jnp.float32,
+    )
+
+
+def placed(x, at, rank):
+    blocks = [jnp.zeros_like(x)] * (LANES // rank)
+    blocks[at] = x
+    return jnp.concatenate(blocks, axis=0)
+
+
+def inverse_factors(sums, rank):
+    row = lax.broadcasted_iota(jnp.int32, (rank, LANES), 0)
+    lane = lax.broadcasted_iota(jnp.int32, (rank, LANES), 1)
+    work = exact_dot(sums[0], placed(sums[0], 0, rank), ((1,), (1,)))
+    work = work + exact_dot(sums[1], placed(sums[1], 2, rank), ((1,), (1,)))
+    work = work + jnp.where((lane == row + rank) | (lane == row + 3 * rank), 1.0, 0.0)
+    first = lane < 2 * rank
+    single = lax.broadcasted_iota(jnp.int32, (rank, 1), 0)
+
+    def eliminate(k, work):
+        col0 = jnp.sum(jnp.where(lane == k, work, 0.0), axis=1, keepdims=True)
+        col1 = jnp.sum(jnp.where(lane == k + 2 * rank, work, 0.0), axis=1, keepdims=True)
+        pivot_row = jnp.sum(jnp.where(row == k, work, 0.0), axis=0, keepdims=True)
+        here = single == k
+        piv0 = jnp.sum(jnp.where(here, col0, 0.0), axis=0, keepdims=True)
+        piv1 = jnp.sum(jnp.where(here, col1, 0.0), axis=0, keepdims=True)
+        ratio = jnp.where(first, col0 / piv0, col1 / piv1)
+        return work - jnp.where(row > k, ratio * pivot_row, 0.0)
+
+    work = lax.fori_loop(0, rank, eliminate, work)
+    diag0 = jnp.sum(jnp.where(lane == row, work, 0.0), axis=1, keepdims=True)
+    diag1 = jnp.sum(jnp.where(lane == row + 2 * rank, work, 0.0), axis=1, keepdims=True)
+    return work * jnp.where(first, 1.0 / jnp.sqrt(diag0), 1.0 / jnp.sqrt(diag1))
+
+
+def kernel(
+    nd,
+    nt,
+    rank,
+    grad_ref,
+    err_ref,
+    start_ref,
+    mom_ref,
+    wgt_ref,
+    vgrad_ref,
+    vmom_ref,
+    vwgt_ref,
+    new_err_ref,
+    new_mom_ref,
+    new_wgt_ref,
+    new_vmom_ref,
+    new_vwgt_ref,
+    high_ref,
+    low_ref,
+    left_part,
+    left_in,
+    left_mid,
+    left_sum,
+    right_part,
+    right_in,
+    right_sum,
+    wgt_all,
+    vec_all,
+    approx_ref,
+    t_send,
+    t_recv,
+    d_send,
+    d_recv,
+    bg_send,
+    bg_recv,
+):
+    mats = high_ref.shape[0]
+    d, t = lax.axis_index("dp"), lax.axis_index("tensor")
+    dp_peers = [lax.rem(d + o, nd) for o in range(1, nd)]
+    t_peers = [lax.rem(t + o, nt) for o in range(1, nt)]
+    t_rows = left_in.shape[2]
+    d_rows = right_in.shape[2]
+    own = wgt_all.shape[2]
+
+    barrier = pltpu.get_barrier_semaphore()
+    for peer in dp_peers:
+        pl.semaphore_signal(barrier, inc=1, device_id=(peer, t), device_id_type=MESH)
+    for peer in t_peers:
+        pl.semaphore_signal(barrier, inc=1, device_id=(d, peer), device_id_type=MESH)
+
+    pending = []
+
+    def push(src, dst, send, recv, device):
+        copy = pltpu.make_async_remote_copy(
+            src_ref=src,
+            dst_ref=dst,
+            send_sem=send,
+            recv_sem=recv,
+            device_id=device,
+            device_id_type=MESH,
+        )
+        copy.start()
+        pending.append(copy)
+        return copy
+
+    def rows_of(x, m):
+        return x[m * rank : (m + 1) * rank]
+
+    for m in range(mats):
+        mixed = grad_ref[0, m].astype(jnp.float32) + err_ref[0, m]
+        high, low = split(mixed)
+        high_ref[m] = high
+        low_ref[m] = low
+    wgt_all[d] = wgt_ref[...] - (step_rate * momentum_coef) * mom_ref[...]
+    vec_all[d] = vgrad_ref[0]
+    right = [jnp.transpose(start_ref[m]) for m in range(mats)]
+
+    background = []
+
+    def push_background():
+        o = len(background)
+        if o < nd - 1:
+            device = (dp_peers[o], t)
+            background.append(
+                push(wgt_all.at[d], wgt_all.at[d], bg_send.at[0, o], bg_recv.at[0, o], device)
+            )
+
+    vector_copies = []
+    for rnd in range(ROUNDS):
+        for m in range(mats):
+            left_part[rnd, m * rank : (m + 1) * rank] = product(
+                right[m], high_ref[m], low_ref[m], ((1,), (1,))
+            )
+        if rnd == 0:
+            pl.semaphore_wait(barrier, nd - 1 + nt - 1)
+        copies = [
+            push(
+                left_part.at[rnd, pl.ds(pl.multiple_of(peer * t_rows, t_rows), t_rows)],
+                left_in.at[rnd, o],
+                t_send.at[rnd, 0, o],
+                t_recv.at[rnd, 0, o],
+                (d, peer),
+            )
+            for o, peer in enumerate(t_peers)
+        ]
+        mine = pl.ds(pl.multiple_of(t * t_rows, t_rows), t_rows)
+        total = left_part[rnd, mine]
+        for o, copy in enumerate(copies):
+            copy.wait_recv()
+            total = total + left_in[rnd, o]
+        left_mid[rnd, d] = total
+        copies = [
+            push(
+                left_mid.at[rnd, d],
+                left_mid.at[rnd, d],
+                d_send.at[rnd, 0, o],
+                d_recv.at[rnd, 0, o],
+                (peer, t),
+            )
+            for o, peer in enumerate(dp_peers)
+        ]
+        if rnd == 0:
+            vector_copies = [
+                push(vgrad_ref.at[0], vec_all.at[d], bg_send.at[1, o], bg_recv.at[1, o], (peer, t))
+                for o, peer in enumerate(dp_peers)
+            ]
+        push_background()
+        for copy in copies:
+            copy.wait_recv()
+        total = left_mid[rnd, 0]
+        for i in range(1, nd):
+            total = total + left_mid[rnd, i]
+        left_sum[rnd, mine] = total
+        copies = [
+            push(
+                left_sum.at[rnd, mine],
+                left_sum.at[rnd, mine],
+                t_send.at[rnd, 1, o],
+                t_recv.at[rnd, 1, o],
+                (d, peer),
+            )
+            for o, peer in enumerate(t_peers)
+        ]
+        for copy in copies:
+            copy.wait_recv()
+        summed = left_sum[rnd]
+        for m in range(mats):
+            right_part[rnd, m * rank : (m + 1) * rank] = product(
+                rows_of(summed, m), high_ref[m], low_ref[m], ((1,), (0,))
+            )
+        copies = [
+            push(
+                right_part.at[rnd, pl.ds(pl.multiple_of(peer * d_rows, d_rows), d_rows)],
+                right_in.at[rnd, o],
+                d_send.at[rnd, 1, o],
+                d_recv.at[rnd, 1, o],
+                (peer, t),
+            )
+            for o, peer in enumerate(dp_peers)
+        ]
+        push_background()
+        push_background()
+        inverse = inverse_factors([rows_of(summed, m) for m in range(mats)], rank)
+        mine = pl.ds(pl.multiple_of(d * d_rows, d_rows), d_rows)
+        total = right_part[rnd, mine]
+        for o, copy in enumerate(copies):
+            copy.wait_recv()
+            total = total + right_in[rnd, o]
+        right_sum[rnd, mine] = total
+        copies = [
+            push(
+                right_sum.at[rnd, mine],
+                right_sum.at[rnd, mine],
+                d_send.at[rnd, 2, o],
+                d_recv.at[rnd, 2, o],
+                (peer, t),
+            )
+            for o, peer in enumerate(dp_peers)
+        ]
+        push_background()
+        if rnd == ROUNDS - 1:
+            basis = [
+                exact_dot(inverse, placed(rows_of(summed, m), 2 * m + 1, rank), ((1,), (0,)))
+                for m in range(mats)
+            ]
+            for copy in vector_copies:
+                copy.wait_recv()
+            vec_total = vec_all[0].astype(jnp.float32)
+            for i in range(1, nd):
+                vec_total = vec_total + vec_all[i].astype(jnp.float32)
+            vmom = momentum_coef * vmom_ref[...] + vec_total * (1.0 / nd)
+            new_vmom_ref[...] = vmom
+            new_vwgt_ref[...] = vwgt_ref[...] - step_rate * vmom
+        for copy in copies:
+            copy.wait_recv()
+        right_all = right_sum[rnd]
+        right = [
+            exact_dot(inverse, placed(rows_of(right_all, m), 2 * m + 1, rank), ((1,), (0,)))
+            for m in range(mats)
+        ]
+
+    while len(background) < nd - 1:
+        push_background()
+    for m in range(mats):
+        b_high, b_low = split(basis[m])
+        r_high, r_low = split(right[m])
+        approx = lax.dot_general(
+            jnp.concatenate([b_high, b_high, b_low, b_low], axis=0),
+            jnp.concatenate([r_high, r_low, r_high, r_low], axis=0),
+            (((0,), (0,)), ((), ())),
+            preferred_element_type=jnp.float32,
+        ) * (1.0 / nd)
+        approx_ref[m] = approx
+        new_err_ref[0, m] = grad_ref[0, m].astype(jnp.float32) + err_ref[0, m] - approx
+        own_rows = pl.ds(pl.multiple_of(d * own, own), own)
+        new_mom_ref[m] = momentum_coef * mom_ref[m] + approx_ref[m, own_rows]
+    for copy in background:
+        copy.wait_recv()
+    for m in range(mats):
+        for i in range(nd):
+            block = slice(i * own, (i + 1) * own)
+            new_wgt_ref[m, block] = (wgt_all[i, m] - step_rate * approx_ref[m, block]).astype(
+                jnp.bfloat16
+            )
+    for copy in pending:
+        copy.wait_send()
+
+
+def one_kernel(
+    nd, nt, gradients, errors, start, moments, weights, vector_grads, vector_moments, vector_weights
+):
+    _, mats, rows, cols = gradients.shape
+    rank = start.shape[2]
+    vrows = vector_grads.shape[1]
+    stack = mats * rank
+    f32, bf16 = jnp.float32, jnp.bfloat16
+    dma = pltpu.SemaphoreType.DMA
+    vmem = pl.BlockSpec(memory_space=pltpu.VMEM)
+    return pl.pallas_call(
+        functools.partial(kernel, nd, nt, rank),
+        out_shape=(
+            jax.ShapeDtypeStruct(errors.shape, f32),
+            jax.ShapeDtypeStruct(moments.shape, f32),
+            jax.ShapeDtypeStruct((mats, rows, cols), bf16),
+            jax.ShapeDtypeStruct(vector_moments.shape, f32),
+            jax.ShapeDtypeStruct(vector_weights.shape, f32),
+        ),
+        in_specs=[vmem] * 8,
+        out_specs=(vmem,) * 5,
+        scratch_shapes=[
+            pltpu.VMEM((mats, rows, cols), bf16),
+            pltpu.VMEM((mats, rows, cols), bf16),
+            pltpu.VMEM((ROUNDS, stack, rows), f32),
+            pltpu.VMEM((ROUNDS, nt - 1, stack // nt, rows), f32),
+            pltpu.VMEM((ROUNDS, nd, stack // nt, rows), f32),
+            pltpu.VMEM((ROUNDS, stack, rows), f32),
+            pltpu.VMEM((ROUNDS, stack, cols), f32),
+            pltpu.VMEM((ROUNDS, nd - 1, stack // nd, cols), f32),
+            pltpu.VMEM((ROUNDS, stack, cols), f32),
+            pltpu.VMEM((nd, mats, rows // nd, cols), f32),
+            pltpu.VMEM((nd, vrows, cols), bf16),
+            pltpu.VMEM((mats, rows, cols), f32),
+            dma((ROUNDS, 2, nt - 1)),
+            dma((ROUNDS, 2, nt - 1)),
+            dma((ROUNDS, 3, nd - 1)),
+            dma((ROUNDS, 3, nd - 1)),
+            dma((2, nd - 1)),
+            dma((2, nd - 1)),
+        ],
+        compiler_params=pltpu.CompilerParams(
+            collective_id=0, has_side_effects=True, vmem_limit_bytes=48 << 20
+        ),
+    )(gradients, errors, start, moments, weights, vector_grads, vector_moments, vector_weights)
+
+
+def fits(nd, nt, mats, rows, rank):
+    stack = mats * rank
+    return (
+        mats == 2
+        and LANES == 4 * rank
+        and nd > 1
+        and nt > 1
+        and stack % (8 * nt) == 0
+        and stack % (8 * nd) == 0
+        and rows % (16 * nd) == 0
+    )
+
+
+def dispatch(nd, nt, *args):
+    gradients, start = args[0], args[2]
+    if fits(nd, nt, gradients.shape[1], gradients.shape[2], start.shape[2]):
+        return one_kernel(nd, nt, *args)
+    return per_device(*args)
+
+
 def solution(mesh):
     in_specs = (
         P("dp", None, None, "tensor"),
@@ -80,5 +438,9 @@
         P(None, "tensor"),
     )
     return jax.shard_map(
-        per_device, mesh=mesh, in_specs=in_specs, out_specs=out_specs, check_vma=False
-    )
+        functools.partial(dispatch, mesh.shape["dp"], mesh.shape["tensor"]),
+        mesh=mesh,
+        in_specs=in_specs,
+        out_specs=out_specs,
+        check_vma=False,
+    )

time: 472 us -> 77.1 us (0.16)
  waiting for transfers between devices: 348 us -> 0 us
  Pallas kernels: 0 us -> 67.9 us
  blocking collectives: 67 us -> 0 us
  other arithmetic: 23.9 us -> 0 us
  matrix products: 13.6 us -> 0 us
  between operations: 13.9 us -> 0.73 us
    psum x4 -> x0, waiting for transfers between devices: 348 us -> none  [the longest x2 208 us: left_basis(): summed = lax.psum(partial_value, ('dp', 'tensor'))]
    pallas_call x0 -> x1, Pallas kernels: none -> 67.9 us  [one_kernel(): pl.pallas_call(functools.partial(kernel, nd, nt, rank), out_shape=(jax.Sh...]
    psum x1 -> x0, blocking collectives: 35.5 us -> none  [per_device(): vector_total = lax.psum(vector_grads[0].astype(jnp.float32), 'dp')]
    all_gather x1 -> x0, blocking collectives: 31.5 us -> none  [update(): regathered = lax.all_gather(fresh_weights, 'dp', axis=1, tiled=True)]
    another operation x12 -> x0, other arithmetic: 22 us -> none  [the longest x7 12 us: basis_from(): factor_low = jnp.linalg.cholesky(gram_mat)]
    dot_general x7 -> x0, matrix products: 12.2 us -> none  [the longest x2 4.91 us: left_basis(): jnp.einsum('mkd,mdr->mkr', mixed, right_f, precision=lax.Precision.HIGHEST)]
  transfers between devices with their start and end apart: 4 -> 0, of which waited for: 4 -> 0; matrix products, arithmetic and copies ran while one was open for 0% -> 0% of each run, Pallas kernels for 0% -> 0%
where the time goes in v1:
time: 77.1 us; the launch traced here: 76.9 us
  Pallas kernels  67.9 us (88%)
  local copies, waits for them, and re-layouts  8.2 us (11%)
    pallas_call x1, Pallas kernels, one_kernel(): pl.pallas_call(functools.partial(kernel, nd, nt, rank), out_shape=(jax.Sh...  67.9 us
    unnamed x22, local copies, waits for them, and re-layouts  5.99 us
    pallas_call x2, local copies, waits for them, and re-layouts, one_kernel(): pl.pallas_call(functools.partial(kernel, nd, nt, rank), out_shape=(jax.Sh...  2.21 us

profile of v1, /device:TPU:0, one launch (start us, length us, event | category | flops | bytes accessed | tf_op | source)
XLA Modules:
  0.0 76.9 jit_solution(5628311714104241345)
XLA Ops:
  0.6 0.0 copy-start.7
  0.6 1.2 %copy.15.start_ref = f32[2,448,32]{2,1,0:T(8,128)S(1)} copy(f32[2,448,32]{1,2,0:T(8,128)} %param.10) | data formatting | bytes 229376 | tf_op args[2]
  1.8 1.2 %copy.13.grad_ref = bf16[1,2,256,448]{3,2,1,0:T(8,128)(2,1)S(1)} copy(bf16[1,2,256,448]{2,3,1,0:T(8,128)(2,1)} %param.8) | data formatting | bytes 917504 | tf_op args[0]
  3.0 0.0 copy-done.7
  3.1 0.0 copy-start.2
  3.1 0.0 copy-start.3
  3.1 0.0 copy-start.4
  3.1 0.0 copy-start.5
  3.1 0.0 copy-start.6
  3.1 0.3 copy.14.err_ref
  3.5 0.5 copy-done.2
  4.0 0.1 copy-done.3
  4.0 0.0 copy-done.4
  4.0 0.0 copy-done.5
  4.0 0.0 copy-done.6
  4.0 67.9 %shard_map.119 = (f32[1,2,256,448]{3,2,1,0:T(8,128)S(1)}, f32[2,32,448]{2,1,0:T(8,128)S(1)}, bf16[2,256,448]{2,1,0:T(8,128)(2,1)S(1)}, f32[5,448]{1,0:T(8,128)S(1)}, f32[5,448]{1,0:T(8,128)S(1)}) custom-call(bf16[1,2,256,448]{3,2,1,0:T(8,128)(2,1)S(1)} %copy.13.grad_ref, f32[1,2,256,448]{3,2,1,0:T(8,128)S(1)} %copy.14.err_ref, ...), custom_call_target="tpu_custom_call" | custom-call | tf_op jit(solution)/shard_map/pallas_call | solution.py:365
  72.0 0.0 copy-start
  72.0 0.8 %copy-done = bf16[2,256,448]{2,1,0:T(8,128)(2,1)} copy-done((bf16[2,256,448]{2,1,0:T(8,128)(2,1)}, bf16[2,256,448]{2,1,0:T(8,128)(2,1)S(1)}, u32[]{:S(2)}) %copy-start) | copy-done | bytes 458776
  72.8 1.2 %copy.16 = f32[1,2,256,448]{2,3,1,0:T(8,128)} copy(f32[1,2,256,448]{3,2,1,0:T(8,128)S(1)} %get-tuple-element.5) | data formatting | bytes 1835008 | tf_op jit(solution)/shard_map/pallas_call | solution.py:365
  74.0 0.0 copy-done.1
  74.0 1.0 %copy.17 = bf16[2,256,448]{1,2,0:T(8,128)(2,1)} copy(bf16[2,256,448]{2,1,0:T(8,128)(2,1)S(1)} %copy-done.1) | data formatting | bytes 917504 | tf_op jit(solution)/shard_map/pallas_call | solution.py:365
  75.0 0.7 copy.21
  75.7 0.6 copy.22
  76.3 0.6 copy.23
  (1 shorter events, 0.0 us)
Async XLA Ops:
  0.6 2.4 %copy-start.7 = (f32[1,2,256,448]{2,3,1,0:T(8,128)S(1)}, f32[1,2,256,448]{2,3,1,0:T(8,128)}, u32[]{:S(2)}) copy-start(f32[1,2,256,448]{2,3,1,0:T(8,128)} %param.9) | copy-start | bytes 2752516
  3.1 0.9 %copy-start.2 = (f32[2,32,448]{2,1,0:T(8,128)S(1)}, f32[2,32,448]{2,1,0:T(8,128)}, u32[]{:S(2)}) copy-start(f32[2,32,448]{2,1,0:T(8,128)} %mom_ref.1) | copy-start | bytes 344068
  3.1 1.0 %copy-start.3 = (f32[2,32,448]{2,1,0:T(8,128)S(1)}, f32[2,32,448]{2,1,0:T(8,128)}, u32[]{:S(2)}) copy-start(f32[2,32,448]{2,1,0:T(8,128)} %wgt_ref.1) | copy-start | bytes 344068
  3.1 1.0 %copy-start.4 = (f32[5,448]{1,0:T(8,128)S(1)}, f32[5,448]{1,0:T(8,128)}, u32[]{:S(2)}) copy-start(f32[5,448]{1,0:T(8,128)} %vmom_ref.1) | copy-start | bytes 26884
  3.1 0.9 %copy-start.5 = (f32[5,448]{1,0:T(8,128)S(1)}, f32[5,448]{1,0:T(8,128)}, u32[]{:S(2)}) copy-start(f32[5,448]{1,0:T(8,128)} %vwgt_ref.1) | copy-start | bytes 26884
  3.1 0.9 %copy-start.6 = (bf16[1,5,448]{2,1,0:T(8,128)(2,1)S(1)}, bf16[1,5,448]{2,1,0:T(8,128)(2,1)}, u32[]{:S(2)}) copy-start(bf16[1,5,448]{2,1,0:T(8,128)(2,1)} %vgrad_ref.1) | copy-start | bytes 13444
  72.0 0.8 %copy-start = (bf16[2,256,448]{2,1,0:T(8,128)(2,1)}, bf16[2,256,448]{2,1,0:T(8,128)(2,1)S(1)}, u32[]{:S(2)}) copy-start(bf16[2,256,448]{2,1,0:T(8,128)(2,1)S(1)} %get-tuple-element.7) | copy-start | bytes 1376260
  72.8 1.2 %copy-start.1 = (bf16[2,256,448]{2,1,0:T(8,128)(2,1)S(1)}, bf16[2,256,448]{2,1,0:T(8,128)(2,1)}, u32[]{:S(2)}) copy-start(bf16[2,256,448]{2,1,0:T(8,128)(2,1)} %copy-done) | copy-start | bytes 1376260

commit v2 on v1

--- a/solution.py
+++ b/solution.py
@@ -124,7 +124,7 @@
     return work * jnp.where(first, 1.0 / jnp.sqrt(diag0), 1.0 / jnp.sqrt(diag1))
 
 
-def kernel(
+def reduce_kernel(
     nd,
     nt,
     rank,
@@ -134,13 +134,10 @@
     mom_ref,
     wgt_ref,
     vgrad_ref,
-    vmom_ref,
-    vwgt_ref,
-    new_err_ref,
-    new_mom_ref,
-    new_wgt_ref,
-    new_vmom_ref,
-    new_vwgt_ref,
+    basis_ref,
+    right_ref,
+    wgt_t_ref,
+    vec_ref,
     high_ref,
     low_ref,
     left_part,
@@ -152,21 +149,25 @@
     right_sum,
     wgt_all,
     vec_all,
-    approx_ref,
     t_send,
     t_recv,
     d_send,
     d_recv,
-    bg_send,
-    bg_recv,
+    w_send,
+    w_recv,
+    v_send,
+    v_recv,
 ):
     mats = high_ref.shape[0]
+    rows = high_ref.shape[2]
     d, t = lax.axis_index("dp"), lax.axis_index("tensor")
     dp_peers = [lax.rem(d + o, nd) for o in range(1, nd)]
     t_peers = [lax.rem(t + o, nt) for o in range(1, nt)]
     t_rows = left_in.shape[2]
     d_rows = right_in.shape[2]
-    own = wgt_all.shape[2]
+    pairs = nd // 2
+    high_at, low_at = d // 2, lax.rem(d, 2)
+    partner = high_at * 2 + 1 - low_at
 
     barrier = pltpu.get_barrier_semaphore()
     for peer in dp_peers:
@@ -197,25 +198,33 @@
         high, low = split(mixed)
         high_ref[m] = high
         low_ref[m] = low
-    wgt_all[d] = wgt_ref[...] - (step_rate * momentum_coef) * mom_ref[...]
-    vec_all[d] = vgrad_ref[0]
-    right = [jnp.transpose(start_ref[m]) for m in range(mats)]
-
-    background = []
-
-    def push_background():
-        o = len(background)
-        if o < nd - 1:
-            device = (dp_peers[o], t)
-            background.append(
-                push(wgt_all.at[d], wgt_all.at[d], bg_send.at[0, o], bg_recv.at[0, o], device)
-            )
-
-    vector_copies = []
+    right = [start_ref[m] for m in range(mats)]
+
+    offsets = sorted(range(1, pairs), key=lambda o: min(o, pairs - o))
+    straight, relayed = [], []
+
+    def push_block(block, sem, device):
+        return push(
+            wgt_all.at[block], wgt_all.at[block], w_send.at[sem], w_recv.at[sem], (device, t)
+        )
+
+    def push_weights(window):
+        if window == 0:
+            relayed.append(push_block(d, 0, partner))
+        if window < len(offsets):
+            o = offsets[window]
+            to = lax.rem(high_at + o, pairs) * 2 + low_at
+            straight.append(push_block(d, 2 * window + 1, to))
+        if 1 <= window <= len(offsets):
+            o = offsets[window - 1]
+            block = lax.rem(high_at + pairs - o, pairs) * 2 + low_at
+            straight[window - 1].wait_recv()
+            relayed.append(push_block(block, 2 * window, partner))
+
     for rnd in range(ROUNDS):
         for m in range(mats):
             left_part[rnd, m * rank : (m + 1) * rank] = product(
-                right[m], high_ref[m], low_ref[m], ((1,), (1,))
+                right[m], high_ref[m], low_ref[m], ((1,), (0,))
             )
         if rnd == 0:
             pl.semaphore_wait(barrier, nd - 1 + nt - 1)
@@ -229,6 +238,10 @@
             )
             for o, peer in enumerate(t_peers)
         ]
+        if rnd == 0:
+            wgt_all[d] = wgt_ref[...] - (step_rate * momentum_coef) * mom_ref[...]
+            vec_all[d] = vgrad_ref[0]
+        push_weights(2 * rnd)
         mine = pl.ds(pl.multiple_of(t * t_rows, t_rows), t_rows)
         total = left_part[rnd, mine]
         for o, copy in enumerate(copies):
@@ -245,12 +258,6 @@
             )
             for o, peer in enumerate(dp_peers)
         ]
-        if rnd == 0:
-            vector_copies = [
-                push(vgrad_ref.at[0], vec_all.at[d], bg_send.at[1, o], bg_recv.at[1, o], (peer, t))
-                for o, peer in enumerate(dp_peers)
-            ]
-        push_background()
         for copy in copies:
             copy.wait_recv()
         total = left_mid[rnd, 0]
@@ -267,12 +274,18 @@
             )
             for o, peer in enumerate(t_peers)
         ]
+        push_weights(2 * rnd + 1)
+        if rnd == ROUNDS - 1:
+            vector_copies = [
+                push(vgrad_ref.at[0], vec_all.at[d], v_send.at[o], v_recv.at[o], (peer, t))
+                for o, peer in enumerate(dp_peers)
+            ]
         for copy in copies:
             copy.wait_recv()
         summed = left_sum[rnd]
         for m in range(mats):
             right_part[rnd, m * rank : (m + 1) * rank] = product(
-                rows_of(summed, m), high_ref[m], low_ref[m], ((1,), (0,))
+                rows_of(summed, m), high_ref[m], low_ref[m], ((1,), (1,))
             )
         copies = [
             push(
@@ -284,8 +297,6 @@
             )
             for o, peer in enumerate(dp_peers)
         ]
-        push_background()
-        push_background()
         inverse = inverse_factors([rows_of(summed, m) for m in range(mats)], rank)
         mine = pl.ds(pl.multiple_of(d * d_rows, d_rows), d_rows)
         total = right_part[rnd, mine]
@@ -303,20 +314,24 @@
             )
             for o, peer in enumerate(dp_peers)
         ]
-        push_background()
         if rnd == ROUNDS - 1:
-            basis = [
-                exact_dot(inverse, placed(rows_of(summed, m), 2 * m + 1, rank), ((1,), (0,)))
-                for m in range(mats)
-            ]
+            for m in range(mats):
+                basis_ref[m * rank : (m + 1) * rank] = exact_dot(
+                    inverse, placed(rows_of(summed, m), 2 * m + 1, rank), ((1,), (0,))
+                )
             for copy in vector_copies:
                 copy.wait_recv()
             vec_total = vec_all[0].astype(jnp.float32)
             for i in range(1, nd):
                 vec_total = vec_total + vec_all[i].astype(jnp.float32)
-            vmom = momentum_coef * vmom_ref[...] + vec_total * (1.0 / nd)
-            new_vmom_ref[...] = vmom
-            new_vwgt_ref[...] = vwgt_ref[...] - step_rate * vmom
+            vec_ref[...] = vec_total
+            for window in range(2 * ROUNDS, len(offsets) + 1):
+                push_weights(window)
+            for copy in relayed:
+                copy.wait_recv()
+            for m in range(mats):
+                whole = jnp.concatenate([wgt_all[i, m] for i in range(nd)], axis=0)
+                wgt_t_ref[m] = jnp.transpose(whole)
         for copy in copies:
             copy.wait_recv()
         right_all = right_sum[rnd]
@@ -324,35 +339,54 @@
             exact_dot(inverse, placed(rows_of(right_all, m), 2 * m + 1, rank), ((1,), (0,)))
             for m in range(mats)
         ]
-
-    while len(background) < nd - 1:
-        push_background()
     for m in range(mats):
-        b_high, b_low = split(basis[m])
-        r_high, r_low = split(right[m])
-        approx = lax.dot_general(
-            jnp.concatenate([b_high, b_high, b_low, b_low], axis=0),
-            jnp.concatenate([r_high, r_low, r_high, r_low], axis=0),
-            (((0,), (0,)), ((), ())),
-            preferred_element_type=jnp.float32,
-        ) * (1.0 / nd)
-        approx_ref[m] = approx
-        new_err_ref[0, m] = grad_ref[0, m].astype(jnp.float32) + err_ref[0, m] - approx
-        own_rows = pl.ds(pl.multiple_of(d * own, own), own)
-        new_mom_ref[m] = momentum_coef * mom_ref[m] + approx_ref[m, own_rows]
-    for copy in background:
-        copy.wait_recv()
-    for m in range(mats):
-        for i in range(nd):
-            block = slice(i * own, (i + 1) * own)
-            new_wgt_ref[m, block] = (wgt_all[i, m] - step_rate * approx_ref[m, block]).astype(
-                jnp.bfloat16
-            )
+        right_ref[m * rank : (m + 1) * rank] = right[m]
     for copy in pending:
         copy.wait_send()
 
 
-def one_kernel(
+def apply_kernel(
+    nd,
+    rank,
+    grad_ref,
+    err_ref,
+    basis_ref,
+    right_ref,
+    wgt_t_ref,
+    vec_ref,
+    mom_ref,
+    vmom_ref,
+    vwgt_ref,
+    new_err_ref,
+    new_mom_ref,
+    new_wgt_ref,
+    new_vmom_ref,
+    new_vwgt_ref,
+):
+    mats, own = mom_ref.shape[0], mom_ref.shape[1]
+    rows = basis_ref.shape[1]
+    d = lax.axis_index("dp")
+    row = lax.broadcasted_iota(jnp.int32, (own, rows), 0)
+    lane = lax.broadcasted_iota(jnp.int32, (own, rows), 1)
+    select = jnp.where(lane == row + d * own, 1.0, 0.0).astype(jnp.bfloat16)
+    dot = functools.partial(lax.dot_general, preferred_element_type=jnp.float32)
+    vmom = momentum_coef * vmom_ref[...] + vec_ref[...] * (1.0 / nd)
+    new_vmom_ref[...] = vmom
+    new_vwgt_ref[...] = vwgt_ref[...] - step_rate * vmom
+    for m in range(mats):
+        b_high, b_low = split(basis_ref[m * rank : (m + 1) * rank])
+        r_high, r_low = split(right_ref[m * rank : (m + 1) * rank])
+        b_all = jnp.concatenate([b_high, b_high, b_low, b_low], axis=0)
+        r_all = jnp.concatenate([r_high, r_low, r_high, r_low], axis=0)
+        approx = dot(r_all, b_all, (((0,), (0,)), ((), ()))) * (1.0 / nd)
+        new_err_ref[0, m] = grad_ref[0, m].astype(jnp.float32) + err_ref[0, m] - approx
+        new_wgt_ref[m] = (wgt_t_ref[m] - step_rate * approx).astype(jnp.bfloat16)
+        b_own = dot(select, b_all, (((1,), (1,)), ((), ()))).astype(jnp.bfloat16)
+        approx_own = dot(b_own, r_all, (((1,), (0,)), ((), ()))) * (1.0 / nd)
+        new_mom_ref[m] = momentum_coef * mom_ref[m] + approx_own
+
+
+def two_kernels(
     nd, nt, gradients, errors, start, moments, weights, vector_grads, vector_moments, vector_weights
 ):
     _, mats, rows, cols = gradients.shape
@@ -362,20 +396,21 @@
     f32, bf16 = jnp.float32, jnp.bfloat16
     dma = pltpu.SemaphoreType.DMA
     vmem = pl.BlockSpec(memory_space=pltpu.VMEM)
-    return pl.pallas_call(
-        functools.partial(kernel, nd, nt, rank),
+    grads_t = jnp.swapaxes(gradients, 2, 3)
+    errors_t = jnp.swapaxes(errors, 2, 3)
+    basis, right, weights_t, vector_sum = pl.pallas_call(
+        functools.partial(reduce_kernel, nd, nt, rank),
         out_shape=(
-            jax.ShapeDtypeStruct(errors.shape, f32),
-            jax.ShapeDtypeStruct(moments.shape, f32),
-            jax.ShapeDtypeStruct((mats, rows, cols), bf16),
-            jax.ShapeDtypeStruct(vector_moments.shape, f32),
-            jax.ShapeDtypeStruct(vector_weights.shape, f32),
+            jax.ShapeDtypeStruct((stack, rows), f32),
+            jax.ShapeDtypeStruct((stack, cols), f32),
+            jax.ShapeDtypeStruct((mats, cols, rows), f32),
+            jax.ShapeDtypeStruct((vrows, cols), f32),
         ),
-        in_specs=[vmem] * 8,
-        out_specs=(vmem,) * 5,
+        in_specs=[vmem] * 6,
+        out_specs=(vmem,) * 4,
         scratch_shapes=[
-            pltpu.VMEM((mats, rows, cols), bf16),
-            pltpu.VMEM((mats, rows, cols), bf16),
+            pltpu.VMEM((mats, cols, rows), bf16),
+            pltpu.VMEM((mats, cols, rows), bf16),
             pltpu.VMEM((ROUNDS, stack, rows), f32),
             pltpu.VMEM((ROUNDS, nt - 1, stack // nt, rows), f32),
             pltpu.VMEM((ROUNDS, nd, stack // nt, rows), f32),
@@ -385,18 +420,49 @@
             pltpu.VMEM((ROUNDS, stack, cols), f32),
             pltpu.VMEM((nd, mats, rows // nd, cols), f32),
             pltpu.VMEM((nd, vrows, cols), bf16),
-            pltpu.VMEM((mats, rows, cols), f32),
             dma((ROUNDS, 2, nt - 1)),
             dma((ROUNDS, 2, nt - 1)),
             dma((ROUNDS, 3, nd - 1)),
             dma((ROUNDS, 3, nd - 1)),
-            dma((2, nd - 1)),
-            dma((2, nd - 1)),
+            dma((nd - 1,)),
+            dma((nd - 1,)),
+            dma((nd - 1,)),
+            dma((nd - 1,)),
         ],
         compiler_params=pltpu.CompilerParams(
-            collective_id=0, has_side_effects=True, vmem_limit_bytes=48 << 20
+            collective_id=0, has_side_effects=True, vmem_limit_bytes=32 << 20
         ),
-    )(gradients, errors, start, moments, weights, vector_grads, vector_moments, vector_weights)
+    )(grads_t, errors_t, jnp.swapaxes(start, 1, 2), moments, weights, vector_grads)
+    new_errors, new_moments, new_weights, new_vmom, new_vwgt = pl.pallas_call(
+        functools.partial(apply_kernel, nd, rank),
+        out_shape=(
+            jax.ShapeDtypeStruct(errors_t.shape, f32),
+            jax.ShapeDtypeStruct(moments.shape, f32),
+            jax.ShapeDtypeStruct((mats, cols, rows), bf16),
+            jax.ShapeDtypeStruct(vector_moments.shape, f32),
+            jax.ShapeDtypeStruct(vector_weights.shape, f32),
+        ),
+        in_specs=[vmem] * 9,
+        out_specs=(vmem,) * 5,
+        compiler_params=pltpu.CompilerParams(vmem_limit_bytes=32 << 20),
+    )(
+        grads_t,
+        errors_t,
+        basis,
+        right,
+        weights_t,
+        vector_sum,
+        moments,
+        vector_moments,
+        vector_weights,
+    )
+    return (
+        jnp.swapaxes(new_errors, 2, 3),
+        new_moments,
+        jnp.swapaxes(new_weights, 1, 2),
+        new_vmom,
+        new_vwgt,
+    )
 
 
 def fits(nd, nt, mats, rows, rank):
@@ -404,18 +470,18 @@
     return (
         mats == 2
         and LANES == 4 * rank
-        and nd > 1
+        and nd % 2 == 0
         and nt > 1
         and stack % (8 * nt) == 0
         and stack % (8 * nd) == 0
-        and rows % (16 * nd) == 0
+        and rows % (8 * nd) == 0
     )
 
 
 def dispatch(nd, nt, *args):
     gradients, start = args[0], args[2]
     if fits(nd, nt, gradients.shape[1], gradients.shape[2], start.shape[2]):
-        return one_kernel(nd, nt, *args)
+        return two_kernels(nd, nt, *args)
     return per_device(*args)
 
 

time: 77.1 us -> 59.3 us (0.77)
  Pallas kernels: 67.9 us -> 52.7 us
  local copies, waits for them, and re-layouts: 8.2 us -> 5.61 us
    pallas_call x1 -> x2, Pallas kernels: 67.9 us -> 52.7 us  [the longest x1 51.1 us: two_kernels(): pl.pallas_call(functools.partial(reduce_kernel, nd, nt, rank), out_shape=...]
    pallas_call x2 -> x0, local copies, waits for them, and re-layouts: 2.21 us -> none  [one_kernel(): pl.pallas_call(functools.partial(kernel, nd, nt, rank), out_shape=(jax.Sh...]
    unnamed x22 -> x18, local copies, waits for them, and re-layouts: 5.99 us -> 5.61 us
where the time goes in v2:
time: 59.3 us; the launch traced here: 59 us
  Pallas kernels  52.7 us (89%)
  local copies, waits for them, and re-layouts  5.61 us (9%)
  between operations  0.68 us (1%)
    pallas_call x1, Pallas kernels, two_kernels(): pl.pallas_call(functools.partial(reduce_kernel, nd, nt, rank), out_shape=...  51.1 us
    unnamed x18, local copies, waits for them, and re-layouts  5.61 us
    pallas_call x1, Pallas kernels, two_kernels(): pl.pallas_call(functools.partial(apply_kernel, nd, rank), out_shape=(jax....  1.56 us

profile of v2, /device:TPU:0, one launch (start us, length us, event | category | flops | bytes accessed | tf_op | source)
XLA Modules:
  0.0 59.0 jit_solution(815009805155281316)
XLA Ops:
  0.6 0.0 copy-start
  0.6 1.2 %copy-done = f32[1,2,256,448]{2,3,1,0:T(8,128)S(1)} copy-done((f32[1,2,256,448]{2,3,1,0:T(8,128)S(1)}, f32[1,2,256,448]{2,3,1,0:T(8,128)}, u32[]{:S(2)}) %copy-start) | copy-done | bytes 917528
  1.8 0.0 copy-start.1
  1.8 1.0 %copy-done.1 = bf16[1,2,256,448]{2,3,1,0:T(8,128)(2,1)S(1)} copy-done((bf16[1,2,256,448]{2,3,1,0:T(8,128)(2,1)S(1)}, bf16[1,2,256,448]{2,3,1,0:T(8,128)(2,1)}, u32[]{:S(2)}) %copy-start.1) | copy-done | bytes 458776
  2.8 0.0 copy-start.2
  2.8 0.9 %copy-done.2 = f32[2,32,448]{2,1,0:T(8,128)S(1)} copy-done((f32[2,32,448]{2,1,0:T(8,128)S(1)}, f32[2,32,448]{2,1,0:T(8,128)}, u32[]{:S(2)}) %copy-start.2) | copy-done | bytes 114712
  3.7 0.0 copy-start.4
  3.7 0.9 %copy-done.4 = f32[2,448,32]{1,2,0:T(8,128)S(1)} copy-done((f32[2,448,32]{1,2,0:T(8,128)S(1)}, f32[2,448,32]{1,2,0:T(8,128)}, u32[]{:S(2)}) %copy-start.4) | copy-done | bytes 114712
  4.6 0.0 copy-start.5
  4.6 0.9 %copy-done.5 = f32[2,32,448]{2,1,0:T(8,128)S(1)} copy-done((f32[2,32,448]{2,1,0:T(8,128)S(1)}, f32[2,32,448]{2,1,0:T(8,128)}, u32[]{:S(2)}) %copy-start.5) | copy-done | bytes 114712
  5.5 0.0 copy-start.8
  5.5 0.7 %copy-done.8 = bf16[1,5,448]{2,1,0:T(8,128)(2,1)S(1)} copy-done((bf16[1,5,448]{2,1,0:T(8,128)(2,1)S(1)}, bf16[1,5,448]{2,1,0:T(8,128)(2,1)}, u32[]{:S(2)}) %copy-start.8) | copy-done | bytes 4504
  6.2 0.0 copy-start.3
  6.2 0.0 copy-start.6
  6.2 0.0 copy-start.7
  6.3 51.1 %shard_map.119 = (f32[64,256]{1,0:T(8,128)S(1)}, f32[64,448]{1,0:T(8,128)S(1)}, f32[2,448,256]{2,1,0:T(8,128)S(1)}, f32[5,448]{1,0:T(8,128)S(1)}) custom-call(bf16[1,2,448,256]{3,2,1,0:T(8,128)(2,1)S(1)} %bitcast.7, f32[1,2,448,256]{3,2,1,0:T(8,128)S(1)} %bitcast.5, f32[2,32,448]{2,1,0:T(8,128)S(1)} %bitcast.9, f32[2,32,448]{2,1,0:T(8,128)S(1)} %copy-done.2, ...), custom_call_target="tpu_custom_call" | custom-call | tf_op jit(solution)/shard_map/pallas_call | solution.py:401
  57.4 0.0 copy-done.3
  57.4 0.0 copy-done.6
  57.4 0.0 copy-done.7
  57.4 1.6 %shard_map.120 = (f32[1,2,448,256]{3,2,1,0:T(8,128)}, f32[2,32,448]{2,1,0:T(8,128)}, bf16[2,448,256]{2,1,0:T(8,128)(2,1)}, f32[5,448]{1,0:T(8,128)}, f32[5,448]{1,0:T(8,128)}) custom-call(bf16[1,2,448,256]{3,2,1,0:T(8,128)(2,1)S(1)} %bitcast.8, f32[1,2,448,256]{3,2,1,0:T(8,128)S(1)} %bitcast.6, f32[64,256]{1,0:T(8,128)S(1)} %get-tuple-element.14.basis_ref, ...), custom_call_target="tpu_custom_call" | custom-call | tf_op jit(solution)/shard_map/pallas_call | solution.py:436
Async XLA Ops:
  0.6 1.2 %copy-start = (f32[1,2,256,448]{2,3,1,0:T(8,128)S(1)}, f32[1,2,256,448]{2,3,1,0:T(8,128)}, u32[]{:S(2)}) copy-start(f32[1,2,256,448]{2,3,1,0:T(8,128)} %param.9) | copy-start | bytes 2752516
  1.8 1.0 %copy-start.1 = (bf16[1,2,256,448]{2,3,1,0:T(8,128)(2,1)S(1)}, bf16[1,2,256,448]{2,3,1,0:T(8,128)(2,1)}, u32[]{:S(2)}) copy-start(bf16[1,2,256,448]{2,3,1,0:T(8,128)(2,1)} %param.8) | copy-start | bytes 1376260
  2.8 0.9 %copy-start.2 = (f32[2,32,448]{2,1,0:T(8,128)S(1)}, f32[2,32,448]{2,1,0:T(8,128)}, u32[]{:S(2)}) copy-start(f32[2,32,448]{2,1,0:T(8,128)} %mom_ref.3) | copy-start | bytes 344068
  3.7 0.9 %copy-start.4 = (f32[2,448,32]{1,2,0:T(8,128)S(1)}, f32[2,448,32]{1,2,0:T(8,128)}, u32[]{:S(2)}) copy-start(f32[2,448,32]{1,2,0:T(8,128)} %param.10) | copy-start | bytes 344068
  4.6 0.9 %copy-start.5 = (f32[2,32,448]{2,1,0:T(8,128)S(1)}, f32[2,32,448]{2,1,0:T(8,128)}, u32[]{:S(2)}) copy-start(f32[2,32,448]{2,1,0:T(8,128)} %wgt_ref.1) | copy-start | bytes 344068
  5.5 0.7 %copy-start.8 = (bf16[1,5,448]{2,1,0:T(8,128)(2,1)S(1)}, bf16[1,5,448]{2,1,0:T(8,128)(2,1)}, u32[]{:S(2)}) copy-start(bf16[1,5,448]{2,1,0:T(8,128)(2,1)} %vgrad_ref.1) | copy-start | bytes 13444
  6.2 51.1 %copy-start.3 = (f32[2,32,448]{2,1,0:T(8,128)S(1)}, f32[2,32,448]{2,1,0:T(8,128)}, u32[]{:S(2)}) copy-start(f32[2,32,448]{2,1,0:T(8,128)} %mom_ref.3) | copy-start | bytes 344068
  6.2 51.1 %copy-start.6 = (f32[5,448]{1,0:T(8,128)S(1)}, f32[5,448]{1,0:T(8,128)}, u32[]{:S(2)}) copy-start(f32[5,448]{1,0:T(8,128)} %vmom_ref.1) | copy-start | bytes 26884
  6.2 51.2 %copy-start.7 = (f32[5,448]{1,0:T(8,128)S(1)}, f32[5,448]{1,0:T(8,128)}, u32[]{:S(2)}) copy-start(f32[5,448]{1,0:T(8,128)} %vwgt_ref.1) | copy-start | bytes 26884

commit v3 on v2

--- a/solution.py
+++ b/solution.py
@@ -128,18 +128,25 @@
     nd,
     nt,
     rank,
+    grad_hbm,
+    err_hbm,
+    start_hbm,
+    mom_hbm,
+    wgt_hbm,
+    vgrad_hbm,
+    basis_ref,
+    right_ref,
+    wgt_t_ref,
+    vec_ref,
     grad_ref,
     err_ref,
     start_ref,
     mom_ref,
     wgt_ref,
-    vgrad_ref,
-    basis_ref,
-    right_ref,
-    wgt_t_ref,
-    vec_ref,
     high_ref,
     low_ref,
+    high_t_ref,
+    low_t_ref,
     left_part,
     left_in,
     left_mid,
@@ -157,6 +164,7 @@
     w_recv,
     v_send,
     v_recv,
+    load_sem,
 ):
     mats = high_ref.shape[0]
     rows = high_ref.shape[2]
@@ -174,6 +182,18 @@
         pl.semaphore_signal(barrier, inc=1, device_id=(peer, t), device_id_type=MESH)
     for peer in t_peers:
         pl.semaphore_signal(barrier, inc=1, device_id=(d, peer), device_id_type=MESH)
+
+    loads = []
+    for m in range(mats):
+        loads.append((start_hbm.at[m], start_ref.at[m]))
+        loads.append((grad_hbm.at[0, m], grad_ref.at[m]))
+        loads.append((err_hbm.at[0, m], err_ref.at[m]))
+    loads += [(mom_hbm, mom_ref), (wgt_hbm, wgt_ref), (vgrad_hbm.at[0], vec_all.at[d])]
+    loads = [
+        pltpu.make_async_copy(src, dst, load_sem.at[i]) for i, (src, dst) in enumerate(loads)
+    ]
+    for load in loads:
+        load.start()
 
     pending = []
 
@@ -193,12 +213,15 @@
     def rows_of(x, m):
         return x[m * rank : (m + 1) * rank]
 
+    right = []
     for m in range(mats):
-        mixed = grad_ref[0, m].astype(jnp.float32) + err_ref[0, m]
+        for load in loads[3 * m : 3 * m + 3]:
+            load.wait()
+        mixed = grad_ref[m].astype(jnp.float32) + err_ref[m]
         high, low = split(mixed)
         high_ref[m] = high
         low_ref[m] = low
-    right = [start_ref[m] for m in range(mats)]
+        right.append(start_ref[m])
 
     offsets = sorted(range(1, pairs), key=lambda o: min(o, pairs - o))
     straight, relayed = [], []
@@ -239,9 +262,14 @@
             for o, peer in enumerate(t_peers)
         ]
         if rnd == 0:
+            for load in loads[3 * mats :]:
+                load.wait()
             wgt_all[d] = wgt_ref[...] - (step_rate * momentum_coef) * mom_ref[...]
-            vec_all[d] = vgrad_ref[0]
         push_weights(2 * rnd)
+        if rnd == 0:
+            for m in range(mats):
+                high_t_ref[m] = jnp.transpose(high_ref[m])
+                low_t_ref[m] = jnp.transpose(low_ref[m])
         mine = pl.ds(pl.multiple_of(t * t_rows, t_rows), t_rows)
         total = left_part[rnd, mine]
         for o, copy in enumerate(copies):
@@ -277,7 +305,7 @@
         push_weights(2 * rnd + 1)
         if rnd == ROUNDS - 1:
             vector_copies = [
-                push(vgrad_ref.at[0], vec_all.at[d], v_send.at[o], v_recv.at[o], (peer, t))
+                push(vec_all.at[d], vec_all.at[d], v_send.at[o], v_recv.at[o], (peer, t))
                 for o, peer in enumerate(dp_peers)
             ]
         for copy in copies:
@@ -285,7 +313,7 @@
         summed = left_sum[rnd]
         for m in range(mats):
             right_part[rnd, m * rank : (m + 1) * rank] = product(
-                rows_of(summed, m), high_ref[m], low_ref[m], ((1,), (1,))
+                rows_of(summed, m), high_t_ref[m], low_t_ref[m], ((1,), (0,))
             )
         copies = [
             push(
@@ -396,6 +424,7 @@
     f32, bf16 = jnp.float32, jnp.bfloat16
     dma = pltpu.SemaphoreType.DMA
     vmem = pl.BlockSpec(memory_space=pltpu.VMEM)
+    hbm = pl.BlockSpec(memory_space=pltpu.HBM)
     grads_t = jnp.swapaxes(gradients, 2, 3)
     errors_t = jnp.swapaxes(errors, 2, 3)
     basis, right, weights_t, vector_sum = pl.pallas_call(
@@ -406,11 +435,18 @@
             jax.ShapeDtypeStruct((mats, cols, rows), f32),
             jax.ShapeDtypeStruct((vrows, cols), f32),
         ),
-        in_specs=[vmem] * 6,
+        in_specs=[hbm] * 6,
         out_specs=(vmem,) * 4,
         scratch_shapes=[
             pltpu.VMEM((mats, cols, rows), bf16),
+            pltpu.VMEM((mats, cols, rows), f32),
+            pltpu.VMEM((mats, rank, cols), f32),
+            pltpu.VMEM(moments.shape, f32),
+            pltpu.VMEM(moments.shape, f32),
             pltpu.VMEM((mats, cols, rows), bf16),
+            pltpu.VMEM((mats, cols, rows), bf16),
+            pltpu.VMEM((mats, rows, cols), bf16),
+            pltpu.VMEM((mats, rows, cols), bf16),
             pltpu.VMEM((ROUNDS, stack, rows), f32),
             pltpu.VMEM((ROUNDS, nt - 1, stack // nt, rows), f32),
             pltpu.VMEM((ROUNDS, nd, stack // nt, rows), f32),
@@ -428,9 +464,10 @@
             dma((nd - 1,)),
             dma((nd - 1,)),
             dma((nd - 1,)),
+            dma((3 * mats + 3,)),
         ],
         compiler_params=pltpu.CompilerParams(
-            collective_id=0, has_side_effects=True, vmem_limit_bytes=32 << 20
+            collective_id=0, has_side_effects=True, vmem_limit_bytes=61 << 20
         ),
     )(grads_t, errors_t, jnp.swapaxes(start, 1, 2), moments, weights, vector_grads)
     new_errors, new_moments, new_weights, new_vmom, new_vwgt = pl.pallas_call(

time: 59.3 us -> 58.8 us (level)
  local copies, waits for them, and re-layouts: 5.61 us -> 3.65 us
  Pallas kernels: 52.7 us -> 54.1 us
    unnamed x18, local copies, waits for them, and re-layouts: 5.61 us -> 3.65 us
    pallas_call x1, Pallas kernels: 51.1 us -> 52.6 us  [two_kernels(): pl.pallas_call(functools.partial(reduce_kernel, nd, nt, rank), out_shape=...]
where the time goes in v3:
time: 58.8 us; the launch traced here: 58.5 us
  Pallas kernels  54.1 us (92%)
  local copies, waits for them, and re-layouts  3.65 us (6%)
  between operations  0.73 us (1%)
    pallas_call x1, Pallas kernels, two_kernels(): pl.pallas_call(functools.partial(reduce_kernel, nd, nt, rank), out_shape=...  52.6 us
    unnamed x18, local copies, waits for them, and re-layouts  3.65 us
    pallas_call x1, Pallas kernels, two_kernels(): pl.pallas_call(functools.partial(apply_kernel, nd, rank), out_shape=(jax....  1.53 us

profile of v3, /device:TPU:0, one launch (start us, length us, event | category | flops | bytes accessed | tf_op | source)
XLA Modules:
  0.0 58.5 jit_solution(10879012330535414802)
XLA Ops:
  0.6 0.0 copy-start
  0.6 0.0 copy-start.1
  0.7 0.0 copy-start.3
  0.7 0.0 copy-start.6
  0.7 0.0 copy-start.7
  0.7 52.6 %shard_map.119 = (f32[64,256]{1,0:T(8,128)}, f32[64,448]{1,0:T(8,128)}, f32[2,448,256]{2,1,0:T(8,128)}, f32[5,448]{1,0:T(8,128)}) custom-call(bf16[1,2,448,256]{3,2,1,0:T(8,128)(2,1)} %bitcast.7, f32[1,2,448,256]{3,2,1,0:T(8,128)} %bitcast.5, f32[2,32,448]{2,1,0:T(8,128)} %bitcast.9, f32[2,32,448]{2,1,0:T(8,128)} %mom_ref.1, f32[2,32,448]{2,1,0:T(8,128)} %wgt_hbm.1, ...), custom_call_target="tpu_custom_call" | custom-call | tf_op jit(solution)/shard_map/pallas_call | solution.py:430
  53.3 0.0 copy-done
  53.3 0.0 copy-done.1
  53.3 0.0 copy-done.3
  53.3 0.0 copy-done.6
  53.3 0.0 copy-done.7
  53.3 0.0 copy-start.2
  53.3 1.2 %copy-done.2 = f32[2,448,256]{2,1,0:T(8,128)S(1)} copy-done((f32[2,448,256]{2,1,0:T(8,128)S(1)}, f32[2,448,256]{2,1,0:T(8,128)}, u32[]{:S(2)}) %copy-start.2) | copy-done | bytes 917528
  54.5 0.0 copy-start.4
  54.5 0.9 %copy-done.4 = f32[64,448]{1,0:T(8,128)S(1)} copy-done((f32[64,448]{1,0:T(8,128)S(1)}, f32[64,448]{1,0:T(8,128)}, u32[]{:S(2)}) %copy-start.4) | copy-done | bytes 114712
  55.4 0.0 copy-start.5
  55.4 0.8 %copy-done.5 = f32[64,256]{1,0:T(8,128)S(1)} copy-done((f32[64,256]{1,0:T(8,128)S(1)}, f32[64,256]{1,0:T(8,128)}, u32[]{:S(2)}) %copy-start.5) | copy-done | bytes 65560
  56.3 0.0 copy-start.8
  56.3 0.7 %copy-done.8 = f32[5,448]{1,0:T(8,128)S(1)} copy-done((f32[5,448]{1,0:T(8,128)S(1)}, f32[5,448]{1,0:T(8,128)}, u32[]{:S(2)}) %copy-start.8) | copy-done | bytes 8984
  57.0 1.5 %shard_map.120 = (f32[1,2,448,256]{3,2,1,0:T(8,128)}, f32[2,32,448]{2,1,0:T(8,128)}, bf16[2,448,256]{2,1,0:T(8,128)(2,1)}, f32[5,448]{1,0:T(8,128)}, f32[5,448]{1,0:T(8,128)}) custom-call(bf16[1,2,448,256]{3,2,1,0:T(8,128)(2,1)S(1)} %bitcast.8, f32[1,2,448,256]{3,2,1,0:T(8,128)S(1)} %bitcast.6, f32[64,256]{1,0:T(8,128)S(1)} %copy-done.5, ...), custom_call_target="tpu_custom_call" | custom-call | tf_op jit(solution)/shard_map/pallas_call | solution.py:473
Async XLA Ops:
  0.6 52.6 %copy-start = (f32[1,2,256,448]{2,3,1,0:T(8,128)S(1)}, f32[1,2,256,448]{2,3,1,0:T(8,128)}, u32[]{:S(2)}) copy-start(f32[1,2,256,448]{2,3,1,0:T(8,128)} %param.9) | copy-start | bytes 2752516
  0.6 52.6 %copy-start.1 = (bf16[1,2,256,448]{2,3,1,0:T(8,128)(2,1)S(1)}, bf16[1,2,256,448]{2,3,1,0:T(8,128)(2,1)}, u32[]{:S(2)}) copy-start(bf16[1,2,256,448]{2,3,1,0:T(8,128)(2,1)} %param.8) | copy-start | bytes 1376260
  0.7 52.6 %copy-start.3 = (f32[2,32,448]{2,1,0:T(8,128)S(1)}, f32[2,32,448]{2,1,0:T(8,128)}, u32[]{:S(2)}) copy-start(f32[2,32,448]{2,1,0:T(8,128)} %mom_ref.1) | copy-start | bytes 344068
  0.7 52.6 %copy-start.6 = (f32[5,448]{1,0:T(8,128)S(1)}, f32[5,448]{1,0:T(8,128)}, u32[]{:S(2)}) copy-start(f32[5,448]{1,0:T(8,128)} %vmom_ref.1) | copy-start | bytes 26884
  0.7 52.6 %copy-start.7 = (f32[5,448]{1,0:T(8,128)S(1)}, f32[5,448]{1,0:T(8,128)}, u32[]{:S(2)}) copy-start(f32[5,448]{1,0:T(8,128)} %vwgt_ref.1) | copy-start | bytes 26884
  53.3 1.2 %copy-start.2 = (f32[2,448,256]{2,1,0:T(8,128)S(1)}, f32[2,448,256]{2,1,0:T(8,128)}, u32[]{:S(2)}) copy-start(f32[2,448,256]{2,1,0:T(8,128)} %get-tuple-element.16.wgt_t_ref) | copy-start | bytes 2752516
  54.5 0.9 %copy-start.4 = (f32[64,448]{1,0:T(8,128)S(1)}, f32[64,448]{1,0:T(8,128)}, u32[]{:S(2)}) copy-start(f32[64,448]{1,0:T(8,128)} %get-tuple-element.15.right_ref) | copy-start | bytes 344068
  55.4 0.8 %copy-start.5 = (f32[64,256]{1,0:T(8,128)S(1)}, f32[64,256]{1,0:T(8,128)}, u32[]{:S(2)}) copy-start(f32[64,256]{1,0:T(8,128)} %get-tuple-element.14.basis_ref) | copy-start | bytes 196612
  56.3 0.7 %copy-start.8 = (f32[5,448]{1,0:T(8,128)S(1)}, f32[5,448]{1,0:T(8,128)}, u32[]{:S(2)}) copy-start(f32[5,448]{1,0:T(8,128)} %get-tuple-element.17.vec_ref) | copy-start | bytes 26884
